TPU v7x, 32 devices: a whole 2x2x4 slice. The times are simulated.
32 devices in a mesh: dp: 4 (over y, x), seq: 8 (over z, core).
Axes of the slice: x: 2, y: 2, z: 4, core: 2. Of those that a mesh axis runs over, the one named last changes fastest.
Arguments:
- tokens: bfloat16 [4, 8192, 1152], P('dp', 'seq'), may hold values from -40 to 40
- d_out: bfloat16 [4, 8192, 1152], P('dp', 'seq'), may hold values from -6 to 6
- frames: int32 [4], P('dp'), may hold values from 16 to 32, as said below
- frame_order: int32 [4, 32], P('dp'), may hold values from 0 to 31, each once within a row
- w_qkv: bfloat16 [1152, 3456], replicated, may hold values from -4 to 4
- w_out: bfloat16 [1152, 1152], replicated, may hold values from -0.1875 to 0.1875
Outputs:
- d_tokens: bfloat16 [4, 8192, 1152], P('dp', 'seq')
- d_w_out: float32 [1152, 1152], P('seq', 'dp')
Inputs may be any that keep to these rules, and one draw needn't show every extreme that they name: Some clip has 32 frames. `frame_order`: each row holds every number of 0 to 31 once.
All inputs are finite; a program needn't handle non-finite values.
Results may differ from a plain program's by a relative error of at most 0.012.
The roundings to bfloat16 on the way count: a program that leaves them out, or rounds other values in their place, can miss the bound.
Values may be sent and summed in bfloat16 or wider, within the bound.
A program may use at most 128 MiB of HBM per device.

v0:
```python
import math

import jax
import jax.numpy as jnp
from jax import lax
from jax.sharding import PartitionSpec as P

H = 16


def layer_stats(tokens):
    values = tokens.astype(jnp.float32)
    center = values - jnp.mean(values, axis=-1, keepdims=True)
    spread = jnp.mean(center * center, axis=-1, keepdims=True)
    inverse = lax.rsqrt(spread + 1e-06)
    return (center * inverse, inverse)


def attend_forward(queries, keys_in, values, live_slots, score_scale):
    scores = (
        jnp.einsum("ciqhe,cjqhe->cqhij", queries, keys_in, preferred_element_type=jnp.float32)
        * score_scale
    )
    scores = jnp.where(live_slots[:, None, None, None, :] > 0.5, scores, -1e30)
    row_max = jnp.max(scores, axis=-1, keepdims=True)
    exponent = jnp.exp(scores - row_max)
    softmax_out = exponent / jnp.sum(exponent, axis=-1, keepdims=True)
    rounded = softmax_out.astype(jnp.bfloat16)
    attended = jnp.einsum(
        "cqhij,cjqhe->ciqhe", rounded, values, preferred_element_type=jnp.float32
    ).astype(jnp.bfloat16)
    return (softmax_out, rounded, attended)


def attend_backward(queries, keys_in, values, softmax_out, rounded, head_grad, score_scale):
    d_values = jnp.einsum(
        "cqhij,ciqhe->cjqhe", rounded, head_grad, preferred_element_type=jnp.float32
    ).astype(jnp.bfloat16)
    prob_grad = jnp.einsum(
        "ciqhe,cjqhe->cqhij", head_grad, values, preferred_element_type=jnp.float32
    )
    inner_sum = jnp.sum(softmax_out * prob_grad, axis=-1, keepdims=True)
    score_grad = (softmax_out * (prob_grad - inner_sum) * score_scale).astype(jnp.bfloat16)
    d_queries = jnp.einsum(
        "cqhij,cjqhe->ciqhe", score_grad, keys_in, preferred_element_type=jnp.float32
    ).astype(jnp.bfloat16)
    d_keys = jnp.einsum(
        "cqhij,ciqhe->cjqhe", score_grad, queries, preferred_element_type=jnp.float32
    ).astype(jnp.bfloat16)
    return (d_queries, d_keys, d_values)


def body(tokens, d_out, frames, frame_order, w_qkv, w_out):
    clip_count, row_count, model_width = tokens.shape
    seq_size = lax.axis_size("seq")
    slot_count = frame_order.shape[1]
    stripe = row_count // slot_count
    patch_count = row_count * seq_size // slot_count
    head_dim = model_width // H
    score_scale = 1.0 / math.sqrt(head_dim)
    live_slots = (frame_order < frames[:, None]).astype(jnp.float32)
    position = lax.axis_index("seq") * row_count + jnp.arange(row_count, dtype=jnp.int32)
    slot_hit = (
        position[:, None] // patch_count == jnp.arange(slot_count, dtype=jnp.int32)[None, :]
    ).astype(jnp.float32)
    row_live = jnp.einsum("rs,cs->cr", slot_hit, live_slots)
    normalized, inverse = layer_stats(tokens)
    normed = normalized.astype(jnp.bfloat16)
    joined = jnp.einsum("crd,dk->crk", normed, w_qkv, preferred_element_type=jnp.float32).astype(
        jnp.bfloat16
    )
    masked = (d_out.astype(jnp.float32) * row_live[:, :, None]).astype(jnp.bfloat16)
    spread_rows = lax.all_to_all(
        joined.reshape(clip_count, row_count // seq_size, seq_size, 3 * model_width),
        "seq",
        split_axis=2,
        concat_axis=1,
        tiled=True,
    )
    head_grid = spread_rows.reshape(clip_count, slot_count, stripe, 3, H, head_dim)
    queries = head_grid[:, :, :, 0]
    keys_in = head_grid[:, :, :, 1]
    values = head_grid[:, :, :, 2]
    softmax_out, rounded, attended = attend_forward(
        queries, keys_in, values, live_slots, score_scale
    )
    returned = lax.all_to_all(
        attended.reshape(clip_count, row_count, 1, model_width),
        "seq",
        split_axis=1,
        concat_axis=2,
        tiled=True,
    )
    attended_rows = returned.reshape(clip_count, row_count, model_width)
    head_rows = jnp.einsum("cre,de->crd", masked, w_out, preferred_element_type=jnp.float32).astype(
        jnp.bfloat16
    )
    grad_out = jnp.einsum("crd,cre->de", attended_rows, masked, preferred_element_type=jnp.float32)
    sent_rows = lax.all_to_all(
        head_rows.reshape(clip_count, row_count // seq_size, seq_size, model_width),
        "seq",
        split_axis=2,
        concat_axis=1,
        tiled=True,
    )
    head_grad = sent_rows.reshape(clip_count, slot_count, stripe, H, head_dim)
    d_queries, d_keys, d_values = attend_backward(
        queries, keys_in, values, softmax_out, rounded, head_grad, score_scale
    )
    stacked = jnp.stack((d_queries, d_keys, d_values), axis=3).reshape(
        clip_count, row_count, 1, 3 * model_width
    )
    returned_grads = lax.all_to_all(stacked, "seq", split_axis=1, concat_axis=2, tiled=True)
    qkv_grad = returned_grads.reshape(clip_count, row_count, 3 * model_width)
    normed_grad = jnp.einsum("crk,dk->crd", qkv_grad, w_qkv, preferred_element_type=jnp.float32)
    mean_grad = jnp.mean(normed_grad, axis=-1, keepdims=True)
    mean_cross = jnp.mean(normed_grad * normalized, axis=-1, keepdims=True)
    d_tokens = (
        masked.astype(jnp.float32) + inverse * (normed_grad - mean_grad - normalized * mean_cross)
    ).astype(jnp.bfloat16)
    share = lax.psum_scatter(
        grad_out.astype(jnp.bfloat16), "dp", scatter_dimension=1, tiled=True
    ).astype(jnp.float32)
    final_out = lax.psum_scatter(share, "seq", scatter_dimension=0, tiled=True)
    return (d_tokens, final_out)


def solution(mesh):
    placed = (P("dp", "seq", None), P("dp", "seq", None), P("dp"), P("dp", None), P(), P())
    return jax.shard_map(
        body,
        mesh=mesh,
        in_specs=placed,
        out_specs=(P("dp", "seq", None), P("seq", "dp")),
        check_vma=False,
    )
```

profile of v0, /device:TPU:0, one launch (start us, length us, event | category | flops | bytes accessed | tf_op | source)
XLA Modules:
  0.0 740.3 jit_solution(13049789444774330318)
XLA Ops:
  7.2 0.0 copy-start
  7.2 0.0 copy-start.2
  7.2 2.2 convert_reduce_fusion
  9.4 0.0 copy-start.9
  9.4 2.4 fusion.20
  11.9 0.0 copy-done.9
  11.9 0.0 copy-start.11
  11.9 0.6 copy-done.11
  12.5 0.0 copy-done.2
  12.5 12.4 %fusion.6 = bf16[1,128,8,3456]{3,2,1,0:T(8,128)(2,1)S(1)} fusion(bf16[1152,3456]{1,0:T(8,128)(2,1)} %param.10, bf16[1,1024,1152]{2,1,0:T(8,128)(2,1)S(1)} %copy-done.2, f32[1024]{0:T(1024)S(1)} %add_rsqrt_fusion, f32[1024]{0:T(1024)S(1)} %broadcast_multiply_fusion.2), kind=kOutput, calls=%fused_computation.13 | convolution fusion | flops 8161984512 | bytes 17408000 | tf_op jit(solution)/shard_map/crd,dk->crk/dot_general | solution.py:69
  24.9 3.7 copy.25
  28.6 6.5 all-to-all-start
  35.8 0.0 copy-done.13
  35.8 0.3 fusion.53
  36.1 0.0 copy-done
  36.1 5.2 fusion.36
  41.3 1.8 copy.28
  43.1 147.9 %all-to-all-done = bf16[1,128,8,3456]{3,1,0,2:T(8,128)(2,1)} async-done(((bf16[1,128,8,3456]{3,1,0,2:T(8,128)(2,1)}), bf16[1,128,8,3456]{3,1,0,2:T(8,128)(2,1)}, u32[]{:S(2)}, u32[]{:S(2)}) %all-to-all-start) | async-done | bytes 7077920 | tf_op jit(solution)/shard_map/all_to_all | solution.py:73
  191.0 3.6 all-to-all-start.1
  194.6 25.5 %reshape.219 = bf16[1,32,32,3,16,72]{5,4,3,2,1,0:T(8,128)(2,1)} reshape(bf16[1,8,128,1,3456]{4,2,1,3,0:T(8,128)(2,1)} %bitcast.7) | data formatting | bytes 14155776 | tf_op jit(solution)/shard_map/reshape | solution.py:80
  220.2 6.1 fusion.67
  226.3 0.0 copy-start.4
  226.3 0.0 copy-start.5
  226.3 8.6 %fusion.30 = f32[32,16,32,32]{2,3,1,0:T(8,128)} fusion(bf16[1,32,32,1,16,72]{5,4,3,2,1,0:T(8,128)(2,1)S(1)} %get-tuple-element.10, bf16[1,32,32,1,16,72]{5,4,3,2,1,0:T(8,128)(2,1)S(1)} %get-tuple-element.9), kind=kOutput, calls=%fused_computation.43 | convolution fusion | flops 75497472 | bytes 6815744 | tf_op jit(solution)/shard_map/ciqhe,cjqhe->cqhij/dot_general | solution.py:21
  234.9 0.0 copy-done.4
  234.9 12.4 %fusion.68 = (f32[32,16,32]{2,1,0:T(8,128)S(1)}, f32[32,16,32,32]{2,3,1,0:T(8,128)}) fusion(f32[32,16,32,32]{2,3,1,0:T(8,128)} %fusion.30, pred[32]{0:T(512)(128)(4,1)S(1)} %compare_bitcast_fusion), kind=kOutput, calls=%fused_computation.87 | output fusion | flops 3145759 | bytes 4259872 | tf_op jit(solution)/shard_map/sub | solution.py:26
  247.3 20.2 %convert_bitcast_fusion = bf16[1,32,32,16,72]{4,1,3,2,0:T(8,128)(2,1)} fusion(bf16[1,32,32,1,16,72]{5,4,3,2,1,0:T(8,128)(2,1)S(1)} %get-tuple-element.8, f32[32,16,32,32]{2,3,1,0:T(8,128)} %get-tuple-element.12, f32[32,16,32]{2,1,0:T(8,128)S(1)} %get-tuple-element.11), kind=kOutput, calls=%fused_computation.32 | convolution fusion | flops 77725696 | bytes 6881280 | tf_op jit(solution)/shard_map/cqhij,cjqhe->ciqhe/dot_general | solution.py:29
  267.4 5.8 copy.37
  273.2 18.0 %reshape.233 = bf16[1,1024,1,1152]{3,2,0,1:T(2,128)(2,1)} reshape(bf16[1,32,32,16,72]{4,3,2,1,0:T(8,128)(2,1)} %copy.37) | data formatting | bytes 4718592 | tf_op jit(solution)/shard_map/reshape | solution.py:88
  291.2 0.5 broadcast.131
  291.7 16.4 %reduce.12 = bf16[1024,1152]{1,0:T(8,128)(2,1)} reduce(bf16[1024,1,1,1152]{3,2,1,0:T(2,128)(2,1)} %bitcast.108, bf16[]{:T(256)} %broadcast.131), dimensions={1,2}, to_apply=%bitcast.95.reduce_sub_computation | reduce | bytes 4718594
  308.1 5.9 reshape.236
  314.1 0.0 all-to-all-done.1
  314.1 5.0 all-to-all-start.3
  319.1 8.4 %reshape.224 = bf16[32,32,16,72]{3,2,1,0:T(8,128)(2,1)} reshape(bf16[1,8,128,1,1152]{4,2,1,3,0:T(8,128)(2,1)S(1)} %bitcast.110) | data formatting | bytes 4718592 | tf_op jit(solution)/shard_map/reshape.30
  327.5 12.0 %fusion.32 = f32[32,16,32,32]{2,3,1,0:T(8,128)} fusion(bf16[1,32,32,1,16,72]{5,4,3,2,1,0:T(8,128)(2,1)} %copy-done.6, bf16[32,32,16,72]{3,2,1,0:T(8,128)(2,1)} %reshape.224), kind=kOutput, calls=%fused_computation.45 | convolution fusion | flops 75497472 | bytes 6815744 | tf_op jit(solution)/shard_map/ciqhe,cjqhe->cqhij/dot_general | solution.py:39
  339.5 18.1 %convert_bitcast_fusion.3 = bf16[1,32,32,1,16,72]{5,1,4,2,3,0:T(8,128)(2,1)} fusion(f32[32,16,32,32]{2,3,1,0:T(8,128)} %fusion.32, bf16[1,32,32,1,16,72]{5,4,3,2,1,0:T(8,128)(2,1)} %copy-done.5, f32[32,16,32,32]{2,3,1,0:T(8,128)} %get-tuple-element.12, f32[32,16,32]{2,1,0:T(8,128)S(1)} %get-tuple-element.11), kind=kOutput, calls=%fused_computation.35 | convolution fusion | flops 80363552 | bytes 8978432 | tf_op jit(solution)/shard_map/cqhij,cjqhe->ciqhe/dot_general | solution.py:44
  357.7 18.9 %convert_bitcast_fusion.2 = bf16[1,32,32,1,16,72]{5,1,4,2,3,0:T(8,128)(2,1)} fusion(f32[32,16,32,32]{2,3,1,0:T(8,128)} %fusion.32, bf16[1,32,32,1,16,72]{5,4,3,2,1,0:T(8,128)(2,1)} %copy-done.4, f32[32,16,32,32]{2,3,1,0:T(8,128)} %get-tuple-element.12, f32[32,16,32]{2,1,0:T(8,128)S(1)} %get-tuple-element.11), kind=kOutput, calls=%fused_computation.34 | convolution fusion | flops 80363552 | bytes 8978432 | tf_op jit(solution)/shard_map/cqhij,ciqhe->cjqhe/dot_general | solution.py:47
  376.5 9.7 %convert_bitcast_fusion.1 = bf16[1,32,32,1,16,72]{5,1,4,2,3,0:T(8,128)(2,1)} fusion(bf16[32,32,16,72]{3,2,1,0:T(8,128)(2,1)} %reshape.224, f32[32,16,32,32]{2,3,1,0:T(8,128)} %get-tuple-element.12, f32[32,16,32]{2,1,0:T(8,128)S(1)} %get-tuple-element.11), kind=kOutput, calls=%fused_computation.33 | convolution fusion | flops 77725696 | bytes 6881280 | tf_op jit(solution)/shard_map/cqhij,ciqhe->cjqhe/dot_general | solution.py:36
  386.2 6.7 pad_maximum_fusion
  392.8 14.7 %copy.33 = bf16[1,32,32,3,16,72]{5,4,3,2,1,0:T(8,128)(2,1)} copy(bf16[1,32,32,3,16,72]{5,1,4,2,3,0:T(8,128)(2,1)S(1)} %pad_maximum_fusion) | data formatting | bytes 14155776 | tf_op jit(solution)/shard_map/stack | solution.py:110
  407.5 45.6 %reshape.232 = bf16[1,1024,1,3456]{3,2,0,1:T(2,128)(2,1)} reshape(bf16[1,32,32,3,16,72]{5,4,3,2,1,0:T(8,128)(2,1)} %copy.33) | data formatting | bytes 14155776 | tf_op jit(solution)/shard_map/reshape | solution.py:110
  453.1 45.0 %reduce.11 = bf16[1024,3456]{1,0:T(8,128)(2,1)} reduce(bf16[1024,1,1,3456]{3,2,1,0:T(2,128)(2,1)} %bitcast.106, bf16[]{:T(256)} %broadcast.131), dimensions={1,2}, to_apply=%bitcast.97.reduce_sub_computation | reduce | bytes 14155778
  498.1 8.9 %reshape.238 = bf16[8,2,221184]{2,1,0:T(2,128)(2,1)} reshape(bf16[1024,3456]{1,0:T(8,128)(2,1)} %reduce.11) | data formatting | bytes 14155776
  507.0 0.0 all-to-all-done.3
  507.0 5.1 all-to-all-start.2
  512.1 0.0 reduce-scatter.5.cloned.1.call-start
  512.1 7.0 reshape.237
  519.2 2.8 copy.46
  522.0 0.2 copy-done.8
  522.3 5.3 convolution_convert_fusion
  527.6 0.0 reduce-scatter.5.cloned.1.call-update
  527.6 0.0 reduce-scatter.7.cloned.1.call-start
  527.6 41.4 %reduce-scatter.5.cloned.1.call-done = bf16[1152,288]{0,1:T(8,128)(2,1)} async-done(((bf16[1152,1152]{0,1:T(8,128)(2,1)}), bf16[1152,288]{0,1:T(8,128)(2,1)}) %reduce-scatter.5.cloned.1.call-update) | async-done | bytes 663568 | tf_op jit(solution)/shard_map/reduce_scatter | solution.py:121
  569.0 2.6 copy.43
  571.6 0.0 reduce-scatter.7.cloned.1.call-update
  571.7 112.9 %all-to-all-done.2 = bf16[8,2,221184]{2,1,0:T(2,128)(2,1)} async-done(((bf16[8,2,221184]{2,1,0:T(2,128)(2,1)}), bf16[8,2,221184]{2,1,0:T(2,128)(2,1)}, u32[]{:S(2)}, u32[]{:S(2)}) %all-to-all-start.2) | async-done | bytes 7077920 | tf_op jit(solution)/shard_map/all_to_all | solution.py:113
  684.6 11.9 %reshape.239 = bf16[1024,1,1,3456]{3,2,1,0:T(2,128)(2,1)} reshape(bf16[8,2,221184]{2,1,0:T(2,128)(2,1)} %all-to-all-done.2) | data formatting | bytes 14155776
  696.5 9.0 %copy.45 = bf16[1,1024,1,3456]{3,1,0,2:T(8,128)(2,1)} copy(bf16[1,1024,1,3456]{3,2,0,1:T(2,128)(2,1)} %bitcast.107) | data formatting | bytes 14155776
  705.5 0.0 copy-done.10
  705.5 19.3 %fusion.15 = (f32[1024]{0:T(1024)S(1)}, f32[1024,1152]{1,0:T(8,128)}) fusion(bf16[1,1024,1152]{2,1,0:T(8,128)(2,1)S(1)} %copy-done.3, f32[1024]{0:T(1024)S(1)} %copy-done.12, f32[1024]{0:T(1024)S(1)} %copy-done.10, bf16[1152,3456]{1,0:T(8,128)(2,1)} %param.10, bf16[1,128,8,1,3456]{4,1,2,3,0:T(8,128)(2,1)} %bitcast.111), kind=kOutput, calls=%fused_computation.22 | convolution fusion | flops 8159624192 | bytes 22130688 | tf_op jit(solution)/shard_map/crk,dk->crd/dot_general | solution.py:115
  724.8 2.6 reduce_sum.58
  727.4 0.0 copy-start.1
  727.5 5.8 fusion.19
  (19 shorter events, 0.1 us)
Async XLA Ops:
  7.2 29.0 %copy-start = (bf16[1152,1152]{1,0:T(8,128)(2,1)S(1)}, bf16[1152,1152]{1,0:T(8,128)(2,1)}, u32[]{:S(2)}) copy-start(bf16[1152,1152]{1,0:T(8,128)(2,1)} %param.11) | copy-start | bytes 7962628
  7.2 5.3 copy-start.2
  9.4 2.5 copy-start.9
  11.9 0.6 copy-start.11
  28.6 7.2 copy-start.13
  28.6 162.4 %all-to-all-start = ((bf16[1,128,8,3456]{3,1,0,2:T(8,128)(2,1)}), bf16[1,128,8,3456]{3,1,0,2:T(8,128)(2,1)}, u32[]{:S(2)}, u32[]{:S(2)}) async-start(bf16[1,128,8,3456]{3,1,0,2:T(8,128)(2,1)} %copy.25), calls=%async_computation | async-start | bytes 14155776 | tf_op jit(solution)/shard_map/all_to_all | solution.py:73
  191.0 123.1 %all-to-all-start.1 = ((bf16[1,128,8,1152]{3,1,0,2:T(8,128)(2,1)}), bf16[1,128,8,1152]{3,1,0,2:T(8,128)(2,1)S(1)}, u32[]{:S(2)}, u32[]{:S(2)}) async-start(bf16[1,128,8,1152]{3,1,0,2:T(8,128)(2,1)} %copy.28), calls=%async_computation.1 | async-start | bytes 4718592 | tf_op jit(solution)/shard_map/all_to_all | solution.py:99
  226.3 8.6 %copy-start.4 = (bf16[1,32,32,1,16,72]{5,4,3,2,1,0:T(8,128)(2,1)}, bf16[1,32,32,1,16,72]{5,4,3,2,1,0:T(8,128)(2,1)S(1)}, u32[]{:S(2)}) copy-start(bf16[1,32,32,1,16,72]{5,4,3,2,1,0:T(8,128)(2,1)S(1)} %get-tuple-element.9) | copy-start | bytes 7077892
  226.3 8.6 %copy-start.5 = (bf16[1,32,32,1,16,72]{5,4,3,2,1,0:T(8,128)(2,1)}, bf16[1,32,32,1,16,72]{5,4,3,2,1,0:T(8,128)(2,1)S(1)}, u32[]{:S(2)}) copy-start(bf16[1,32,32,1,16,72]{5,4,3,2,1,0:T(8,128)(2,1)S(1)} %get-tuple-element.10) | copy-start | bytes 7077892
  226.3 20.9 %copy-start.6 = (bf16[1,32,32,1,16,72]{5,4,3,2,1,0:T(8,128)(2,1)}, bf16[1,32,32,1,16,72]{5,4,3,2,1,0:T(8,128)(2,1)S(1)}, u32[]{:S(2)}) copy-start(bf16[1,32,32,1,16,72]{5,4,3,2,1,0:T(8,128)(2,1)S(1)} %get-tuple-element.8) | copy-start | bytes 7077892
  314.1 192.9 %all-to-all-start.3 = ((bf16[8,2,73728]{2,1,0:T(2,128)(2,1)}), bf16[8,2,73728]{2,1,0:T(2,128)(2,1)}, u32[]{:S(2)}, u32[]{:S(2)}) async-start(bf16[8,2,73728]{2,1,0:T(2,128)(2,1)} %reshape.236), calls=%async_computation.3 | async-start | bytes 4718592 | tf_op jit(solution)/shard_map/all_to_all | solution.py:87
  376.5 9.7 %copy-start.7 = (bf16[1,32,32,1,16,72]{5,1,4,2,3,0:T(8,128)(2,1)S(1)}, bf16[1,32,32,1,16,72]{5,1,4,2,3,0:T(8,128)(2,1)}, u32[]{:S(2)}) copy-start(bf16[1,32,32,1,16,72]{5,1,4,2,3,0:T(8,128)(2,1)} %convert_bitcast_fusion.3) | copy-start | bytes 7077892
  507.0 177.6 %all-to-all-start.2 = ((bf16[8,2,221184]{2,1,0:T(2,128)(2,1)}), bf16[8,2,221184]{2,1,0:T(2,128)(2,1)}, u32[]{:S(2)}, u32[]{:S(2)}) async-start(bf16[8,2,221184]{2,1,0:T(2,128)(2,1)} %reshape.238), calls=%async_computation.2 | async-start | bytes 14155776 | tf_op jit(solution)/shard_map/all_to_all | solution.py:113
  512.1 56.9 %reduce-scatter.5.cloned.1.call-start = ((), (), s32[]{:S(2)}) async-start(), calls=%async_computation.6 | async-start | bytes 3317760 | tf_op jit(solution)/shard_map/reduce_scatter | solution.py:121
  519.2 3.1 copy-start.8
  527.6 205.7 %reduce-scatter.7.cloned.1.call-start = ((), (), s32[]{:S(2)}) async-start(), calls=%async_computation.7 | async-start | bytes 1990656
  696.5 9.0 %copy-start.3 = (bf16[1,1024,1152]{2,1,0:T(8,128)(2,1)S(1)}, bf16[1,1024,1152]{2,1,0:T(8,128)(2,1)}, u32[]{:S(2)}) copy-start(bf16[1,1024,1152]{2,1,0:T(8,128)(2,1)} %param.6) | copy-start | bytes 7077892
  696.5 9.0 %copy-start.10 = (f32[1024]{0:T(1024)S(1)}, f32[1024]{0:T(1024)}, u32[]{:S(2)}) copy-start(f32[1024]{0:T(1024)} %copy-done.9) | copy-start | bytes 12292
  696.5 9.0 %copy-start.12 = (f32[1024]{0:T(1024)S(1)}, f32[1024]{0:T(1024)}, u32[]{:S(2)}) copy-start(f32[1024]{0:T(1024)} %copy-done.11) | copy-start | bytes 12292
  727.4 5.9 copy-start.1
Sparse Core Ops, SparseCore 0:
  527.7 41.2 reduce-scatter.4
  571.9 81.3 reduce-scatter.6
where the time goes:
time: 746 us; the launch traced here: 740 us
  waiting for transfers between devices  302 us (40%)
  local copies, waits for them, and re-layouts  179 us (24%)
  matrix products  130 us (17%)
  other arithmetic  93.5 us (13%)
  starting transfers between devices  20.3 us (3%)
  between operations  15.1 us (2%)
    all_to_all x1, waiting for transfers between devices, body(): lax.all_to_all(joined.reshape(clip_count, row_count // seq_size, seq_size...  148 us
    all_to_all x1, waiting for transfers between devices, body(): lax.all_to_all(stacked, 'seq', split_axis=1, concat_axis=2, tiled=True)  113 us
    unnamed x2, other arithmetic  61.4 us
    unnamed x36, local copies, waits for them, and re-layouts  49.7 us
    reshape x1, local copies, waits for them, and re-layouts, body(): jnp.stack((d_queries, d_keys, d_values), axis=3)  45.6 us
    reduce_scatter x1, waiting for transfers between devices, body(): lax.psum_scatter(grad_out.astype(jnp.bfloat16), 'dp', scatter_dimension=1...  41.4 us
    reshape x1, local copies, waits for them, and re-layouts, body(): spread_rows.reshape(clip_count, slot_count, stripe, 3, H, head_dim)  25.5 us
    dot_general x1, matrix products, attend_forward(): jnp.einsum('cqhij,cjqhe->ciqhe', rounded, values, preferred_element_type=...  20.2 us
  transfers between devices with their start and end apart: 6, of which 3 were waited for; matrix products, arithmetic and copies ran while one was open for 51% of the time, Pallas kernels for 0%

commit v1 on v0

v1 whole, which is shorter than its diff:
```python
import functools
import math

import jax
import jax.numpy as jnp
from jax import lax
from jax.experimental import pallas as pl
from jax.experimental.pallas import tpu as pltpu
from jax.sharding import PartitionSpec as P

H = 16
LANES = 128
GROUP = 8
NT = (((1,), (1,)), ((), ()))
TN = (((0,), (0,)), ((), ()))


def dot(a, b, dims=(((1,), (0,)), ((), ()))):
    return lax.dot_general(a, b, dims, preferred_element_type=jnp.float32)


def attend(joined, head_grad, mask, attended, qkv_grad, width, score_scale):
    head_dim = width // H
    column = lax.broadcasted_iota(jnp.int32, (1, 2 * LANES), 1)
    pending = [{}, {}, {}, {}]
    for h in range(H):
        low, high = h * head_dim, (h + 1) * head_dim
        first, last = low // LANES, -(-high // LANES)
        start, size = first * LANES, (last - first) * LANES
        keep = jnp.where(
            (column[:, :size] >= low - start) & (column[:, :size] < high - start), 1.0, 0.0
        ).astype(jnp.bfloat16)
        q = joined[:, start : start + size] * keep
        k = joined[:, width + start : width + start + size] * keep
        v = joined[:, 2 * width + start : 2 * width + start + size] * keep
        g = head_grad[:, start : start + size] * keep
        scores = dot(q, k, NT) * score_scale + mask
        exponent = jnp.exp(scores - jnp.max(scores, axis=-1, keepdims=True))
        probs = exponent * (1.0 / jnp.sum(exponent, axis=-1, keepdims=True))
        rounded = probs.astype(jnp.bfloat16)
        prob_grad = dot(g, v, NT)
        inner = jnp.sum(probs * prob_grad, axis=-1, keepdims=True)
        score_grad = (probs * (prob_grad - inner) * score_scale).astype(jnp.bfloat16)
        results = (
            dot(rounded, v),
            dot(score_grad, k),
            dot(score_grad, q, TN),
            dot(rounded, g, TN),
        )
        for which, result in enumerate(results):
            for tile in range(first, last):
                piece = result[:, (tile - first) * LANES : (tile - first + 1) * LANES]
                held = pending[which].pop(tile, None)
                piece = piece if held is None else held + piece
                if (tile + 1) * LANES <= high:
                    piece = piece.astype(jnp.bfloat16)
                    if which == 0:
                        attended[:, tile * LANES : (tile + 1) * LANES] = piece
                    else:
                        at = (which - 1) * width + tile * LANES
                        qkv_grad[:, at : at + LANES] = piece
                else:
                    pending[which][tile] = piece


def kernel(
    score_scale,
    tokens_ref,
    d_out_ref,
    live_ref,
    mask_ref,
    w_qkv_ref,
    w_out_ref,
    d_tokens_ref,
    grad_ref,
    joined,
    head_grad,
    attended,
    qkv_grad,
):
    rows, width = attended.shape
    values = tokens_ref[...].astype(jnp.float32).reshape(rows, width)
    center = values - jnp.mean(values, axis=-1, keepdims=True)
    inverse = lax.rsqrt(jnp.mean(center * center, axis=-1, keepdims=True) + 1e-06)
    normalized = center * inverse
    normed = normalized.astype(jnp.bfloat16)
    masked_wide = d_out_ref[...].astype(jnp.float32).reshape(rows, width) * live_ref[...]
    masked = masked_wide.astype(jnp.bfloat16)
    joined[...] = dot(normed, w_qkv_ref[...]).astype(jnp.bfloat16)
    head_grad[...] = dot(masked, w_out_ref[...], NT).astype(jnp.bfloat16)
    attend(joined, head_grad, mask_ref[...], attended, qkv_grad, width, score_scale)
    term = dot(attended[...], masked, TN)

    @pl.when(pl.program_id(0) == 0)
    def _():
        grad_ref[...] = term

    @pl.when(pl.program_id(0) != 0)
    def _():
        grad_ref[...] += term

    normed_grad = dot(qkv_grad[...], w_qkv_ref[...], NT)
    mean_grad = jnp.mean(normed_grad, axis=-1, keepdims=True)
    mean_cross = jnp.mean(normed_grad * normalized, axis=-1, keepdims=True)
    result = masked_wide + inverse * (normed_grad - mean_grad - normalized * mean_cross)
    d_tokens_ref[...] = result.reshape(d_tokens_ref.shape).astype(jnp.bfloat16)


def local_part(tokens, d_out, live_slots, w_qkv, w_out):
    slot_count, stripe, width = tokens.shape
    group = min(GROUP, stripe)
    rows = slot_count * group
    steps = stripe // group
    at = jnp.arange(rows, dtype=jnp.int32)
    live_rows = jnp.repeat(live_slots, group)
    mask = jnp.where(
        (at[:, None] % group == at[None, :] % group) & (live_rows[None, :] > 0.5), 0.0, -1e30
    ).astype(jnp.float32)
    if steps == 1:
        tokens, d_out = tokens.reshape(rows, width), d_out.reshape(rows, width)
        moving = pl.BlockSpec((rows, width), lambda i: (0, 0))
    else:
        moving = pl.BlockSpec((slot_count, group, width), lambda i: (0, i, 0))

    def whole(shape):
        return pl.BlockSpec(shape, lambda i: (0, 0), pipeline_mode=pl.Buffered(1))

    d_tokens, grad = pl.pallas_call(
        functools.partial(kernel, 1.0 / math.sqrt(width // H)),
        grid=(steps,),
        in_specs=[
            moving,
            moving,
            whole((rows, 1)),
            whole((rows, rows)),
            whole(w_qkv.shape),
            whole(w_out.shape),
        ],
        out_specs=[moving, whole((width, width))],
        out_shape=[
            jax.ShapeDtypeStruct(tokens.shape, jnp.bfloat16),
            jax.ShapeDtypeStruct((width, width), jnp.float32),
        ],
        scratch_shapes=[
            pltpu.VMEM((rows, 3 * width), jnp.bfloat16),
            pltpu.VMEM((rows, width), jnp.bfloat16),
            pltpu.VMEM((rows, width), jnp.bfloat16),
            pltpu.VMEM((rows, 3 * width), jnp.bfloat16),
        ],
        compiler_params=pltpu.CompilerParams(
            dimension_semantics=("arbitrary",), vmem_limit_bytes=60 * 2**20
        ),
    )(tokens, d_out, live_rows[:, None], mask, w_qkv, w_out)
    return d_tokens.reshape(slot_count, stripe, width), grad


def body(tokens, d_out, frames, frame_order, w_qkv, w_out):
    _, row_count, width = tokens.shape
    seq_size = lax.axis_size("seq")
    slot_count = frame_order.shape[1]
    stripe = row_count // slot_count
    patch_count = row_count * seq_size // slot_count
    slots = max(1, row_count // patch_count)
    piece = row_count // slots // seq_size
    live_slots = (frame_order[0] < frames[0]).astype(jnp.float32)

    def spread(rows):
        sent = rows.reshape(slots, seq_size, piece, width)
        got = lax.all_to_all(sent, "seq", split_axis=1, concat_axis=0, tiled=True)
        return got.reshape(slot_count, stripe, width)

    d_rows, grad_out = local_part(spread(tokens), spread(d_out), live_slots, w_qkv, w_out)
    back = d_rows.reshape(seq_size * slots, 1, piece, width)
    d_tokens = lax.all_to_all(back, "seq", split_axis=0, concat_axis=1, tiled=True)
    share = lax.psum_scatter(
        grad_out.astype(jnp.bfloat16), "dp", scatter_dimension=1, tiled=True
    ).astype(jnp.float32)
    final_out = lax.psum_scatter(share, "seq", scatter_dimension=0, tiled=True)
    return (d_tokens.reshape(tokens.shape), final_out)


def solution(mesh):
    placed = (P("dp", "seq", None), P("dp", "seq", None), P("dp"), P("dp", None), P(), P())
    return jax.shard_map(
        body,
        mesh=mesh,
        in_specs=placed,
        out_specs=(P("dp", "seq", None), P("seq", "dp")),
        check_vma=False,
    )
```

time: 746 us -> 296 us (0.40)
  local copies, waits for them, and re-layouts: 179 us -> 14.1 us
  matrix products: 130 us -> 0 us
  waiting for transfers between devices: 302 us -> 174 us
  other arithmetic: 93.5 us -> 4.96 us
  Pallas kernels: 0 us -> 74.1 us
    all_to_all x4 -> x3, waiting for transfers between devices: 261 us -> 129 us  [the longest x2 103 us: spread(): got = lax.all_to_all(sent, 'seq', split_axis=1, concat_axis=0, tiled=True)]
    dot_general x11 -> x0, matrix products: 130 us -> none  [the longest x1 20.2 us: attend_forward(): jnp.einsum('cqhij,cjqhe->ciqhe', rounded, values, preferred_element_type=...]
    reshape x5 -> x2, local copies, waits for them, and re-layouts: 94.7 us -> 6.65 us  [spread(): sent = rows.reshape(slots, seq_size, piece, width)]
    pallas_call x0 -> x1, Pallas kernels: none -> 74.1 us  [local_part(): pl.pallas_call(functools.partial(kernel, 1.0 / math.sqrt(width // H)), gr...]
    unnamed x2 -> x0, other arithmetic: 61.4 us -> none
    unnamed x36 -> x6, local copies, waits for them, and re-layouts: 49.7 us -> 4.76 us
    unnamed x3, waiting for transfers between devices: 0.03 us -> 35.3 us
    reduce_scatter x1, waiting for transfers between devices: 41.4 us -> 9.05 us  [body(): final_out = lax.psum_scatter(share, 'seq', scatter_dimension=0, tiled=True)]
  transfers between devices with their start and end apart: 6 -> 5, of which waited for: 3 -> 5; matrix products, arithmetic and copies ran while one was open for 51% -> 3% of each run, Pallas kernels for 0% -> 0%
where the time goes in v1:
time: 296 us
  waiting for transfers between devices  174 us (59%)
  Pallas kernels  74.1 us (25%)
  between operations  14.7 us (5%)
  starting transfers between devices  14.4 us (5%)
  local copies, waits for them, and re-layouts  14.1 us (5%)
  other arithmetic  4.96 us (2%)
    all_to_all x2, waiting for transfers between devices, spread(): got = lax.all_to_all(sent, 'seq', split_axis=1, concat_axis=0, tiled=True)  103 us
    pallas_call x1, Pallas kernels, local_part(): pl.pallas_call(functools.partial(kernel, 1.0 / math.sqrt(width // H)), gr...  74.1 us
    unnamed x3, waiting for transfers between devices  35.3 us
    all_to_all x1, waiting for transfers between devices, body(): lax.all_to_all(back, 'seq', split_axis=0, concat_axis=1, tiled=True)  25.8 us
    all_to_all x2, starting transfers between devices, spread(): got = lax.all_to_all(sent, 'seq', split_axis=1, concat_axis=0, tiled=True)  10.7 us
    reduce_scatter x1, waiting for transfers between devices, body(): final_out = lax.psum_scatter(share, 'seq', scatter_dimension=0, tiled=True)  9.05 us
    reshape x2, local copies, waits for them, and re-layouts, spread(): sent = rows.reshape(slots, seq_size, piece, width)  6.65 us
  transfers between devices with their start and end apart: 5, of which 5 were waited for; matrix products, arithmetic and copies ran while one was open for 3% of the time, Pallas kernels for 0%

profile of v1, /device:TPU:0, one launch (start us, length us, event | category | flops | bytes accessed | tf_op | source)
XLA Modules:
  0.0 295.8 jit_solution(976856738222326953)
XLA Ops:
  7.2 3.3 %copy.15 = bf16[4,8,32,1152]{3,2,0,1:T(8,128)(2,1)} copy(bf16[4,8,32,1152]{3,2,1,0:T(8,128)(2,1)} %bitcast.29) | data formatting | bytes 4718592 | tf_op jit(solution)/shard_map/reshape | solution.py:168
  10.5 6.4 %all-to-all-start = ((bf16[4,8,32,1152]{3,2,0,1:T(8,128)(2,1)}), bf16[4,8,32,1152]{3,2,0,1:T(8,128)(2,1)S(1)}, u32[]{:S(2)}, u32[]{:S(2)}) async-start(bf16[4,8,32,1152]{3,2,0,1:T(8,128)(2,1)} %copy.15), calls=%async_computation | async-start | bytes 4718592 | tf_op jit(solution)/shard_map/all_to_all | solution.py:169
  16.8 3.3 %copy.16 = bf16[4,8,32,1152]{3,2,0,1:T(8,128)(2,1)} copy(bf16[4,8,32,1152]{3,2,1,0:T(8,128)(2,1)} %bitcast.30) | data formatting | bytes 4718592 | tf_op jit(solution)/shard_map/reshape | solution.py:168
  20.2 0.0 copy-start.1
  20.2 51.3 %all-to-all-done = bf16[4,8,32,1152]{3,2,0,1:T(8,128)(2,1)S(1)} async-done(((bf16[4,8,32,1152]{3,2,0,1:T(8,128)(2,1)}), bf16[4,8,32,1152]{3,2,0,1:T(8,128)(2,1)S(1)}, u32[]{:S(2)}, u32[]{:S(2)}) %all-to-all-start) | async-done | bytes 2359328 | tf_op jit(solution)/shard_map/all_to_all | solution.py:169
  71.5 0.0 copy-start
  71.5 4.4 %all-to-all-start.1 = ((bf16[4,8,32,1152]{3,2,0,1:T(8,128)(2,1)}), bf16[4,8,32,1152]{3,2,0,1:T(8,128)(2,1)}, u32[]{:S(2)}, u32[]{:S(2)}) async-start(bf16[4,8,32,1152]{3,2,0,1:T(8,128)(2,1)} %copy.16), calls=%async_computation.1 | async-start | bytes 4718592 | tf_op jit(solution)/shard_map/all_to_all | solution.py:169
  75.9 0.0 reduce-scatter.7.cloned.1.call-start
  76.6 0.0 copy-done
  76.6 0.0 copy-done.1
  76.6 0.1 broadcast_in_dim.16
  76.7 0.1 gt.17
  76.8 0.1 broadcast_in_dim.15
  76.9 0.8 broadcast_in_dim_reshape.5.live_ref
  77.6 0.8 and_select_fusion.mask_ref
  78.4 52.1 %all-to-all-done.1 = bf16[4,8,32,1152]{3,2,0,1:T(8,128)(2,1)} async-done(((bf16[4,8,32,1152]{3,2,0,1:T(8,128)(2,1)}), bf16[4,8,32,1152]{3,2,0,1:T(8,128)(2,1)}, u32[]{:S(2)}, u32[]{:S(2)}) %all-to-all-start.1) | async-done | bytes 2359328 | tf_op jit(solution)/shard_map/all_to_all | solution.py:169
  130.5 74.1 %shard_map.77 = (bf16[32,32,1152]{2,1,0:T(8,128)(2,1)}, f32[1152,1152]{1,0:T(8,128)}) custom-call(bf16[32,32,1152]{2,1,0:T(8,128)(2,1)} %bitcast.28, bf16[32,32,1152]{2,1,0:T(8,128)(2,1)} %bitcast.9.d_out_ref, f32[256,1]{1,0:T(8,128)} %broadcast_in_dim_reshape.5.live_ref, f32[256,256]{1,0:T(8,128)} %and_select_fusion.mask_ref, bf16[1152,3456]{1,0:T(8,128)(2,1)} %w_qkv_ref.1, ...), custom_call_target="tpu_custom_call" | custom-call | tf_op jit(solution)/shard_map/pallas_call | solution.py:128
  204.6 2.8 convert_element_type.14
  207.4 3.3 %copy.20 = bf16[1152,1152]{0,1:T(8,128)(2,1)} copy(bf16[1152,1152]{1,0:T(8,128)(2,1)S(1)} %convert_element_type.14) | data formatting | bytes 5308416
  210.6 0.0 reduce-scatter.7.cloned.1.call-update
  210.7 3.6 %all-to-all-start.2 = ((bf16[32,1,32,1152]{3,2,1,0:T(8,128)(2,1)}), bf16[32,1,32,1152]{3,2,1,0:T(8,128)(2,1)S(1)}, u32[]{:S(2)}, u32[]{:S(2)}) async-start(bf16[32,1,32,1152]{3,2,1,0:T(8,128)(2,1)} %bitcast.31), calls=%async_computation.2 | async-start | bytes 4718592 | tf_op jit(solution)/shard_map/all_to_all | solution.py:174
  214.3 0.0 reduce-scatter.5.cloned.1.call-start
  214.4 35.2 %reduce-scatter.7.cloned.1.call-done = bf16[288,1152]{1,0:T(8,128)(2,1)} async-done(((bf16[1152,1152]{1,0:T(8,128)(2,1)}), bf16[288,1152]{1,0:T(8,128)(2,1)}) %reduce-scatter.7.cloned.1.call-update) | async-done | bytes 663568
  249.6 1.5 copy.21
  251.1 1.3 convert_element_type.15
  252.4 0.0 reduce-scatter.5.cloned.1.call-update
  252.4 25.8 %all-to-all-done.2 = bf16[32,1,32,1152]{3,2,1,0:T(8,128)(2,1)S(1)} async-done(((bf16[32,1,32,1152]{3,2,1,0:T(8,128)(2,1)}), bf16[32,1,32,1152]{3,2,1,0:T(8,128)(2,1)S(1)}, u32[]{:S(2)}, u32[]{:S(2)}) %all-to-all-start.2) | async-done | bytes 2359328 | tf_op jit(solution)/shard_map/all_to_all | solution.py:174
  278.3 1.7 copy.19
  279.9 9.0 %reduce-scatter.5.cloned.1.call-done = f32[144,288]{1,0:T(8,128)} async-done(((f32[1152,288]{1,0:T(8,128)}), f32[144,288]{1,0:T(8,128)}) %reduce-scatter.5.cloned.1.call-update) | async-done | bytes 165904 | tf_op jit(solution)/shard_map/reduce_scatter | solution.py:178
  (2 shorter events, 0.0 us)
Async XLA Ops:
  10.5 61.0 %all-to-all-start = ((bf16[4,8,32,1152]{3,2,0,1:T(8,128)(2,1)}), bf16[4,8,32,1152]{3,2,0,1:T(8,128)(2,1)S(1)}, u32[]{:S(2)}, u32[]{:S(2)}) async-start(bf16[4,8,32,1152]{3,2,0,1:T(8,128)(2,1)} %copy.15), calls=%async_computation | async-start | bytes 4718592 | tf_op jit(solution)/shard_map/all_to_all | solution.py:169
  20.2 56.4 %copy-start.1 = (s32[1,32]{1,0:T(1,128)S(1)}, s32[1,32]{1,0:T(1,128)}, u32[]{:S(2)}) copy-start(s32[1,32]{1,0:T(1,128)} %param.9) | copy-start | bytes 388
  71.5 5.1 %copy-start = (bf16[4,8,32,1152]{3,2,0,1:T(8,128)(2,1)}, bf16[4,8,32,1152]{3,2,0,1:T(8,128)(2,1)S(1)}, u32[]{:S(2)}) copy-start(bf16[4,8,32,1152]{3,2,0,1:T(8,128)(2,1)S(1)} %all-to-all-done) | copy-start | bytes 7077892
  71.5 59.0 %all-to-all-start.1 = ((bf16[4,8,32,1152]{3,2,0,1:T(8,128)(2,1)}), bf16[4,8,32,1152]{3,2,0,1:T(8,128)(2,1)}, u32[]{:S(2)}, u32[]{:S(2)}) async-start(bf16[4,8,32,1152]{3,2,0,1:T(8,128)(2,1)} %copy.16), calls=%async_computation.1 | async-start | bytes 4718592 | tf_op jit(solution)/shard_map/all_to_all | solution.py:169
  75.9 173.7 %reduce-scatter.7.cloned.1.call-start = ((), (), s32[]{:S(2)}) async-start(), calls=%async_computation.6 | async-start | bytes 3317760
  210.7 67.6 %all-to-all-start.2 = ((bf16[32,1,32,1152]{3,2,1,0:T(8,128)(2,1)}), bf16[32,1,32,1152]{3,2,1,0:T(8,128)(2,1)S(1)}, u32[]{:S(2)}, u32[]{:S(2)}) async-start(bf16[32,1,32,1152]{3,2,1,0:T(8,128)(2,1)} %bitcast.31), calls=%async_computation.2 | async-start | bytes 4718592 | tf_op jit(solution)/shard_map/all_to_all | solution.py:174
  214.3 74.7 %reduce-scatter.5.cloned.1.call-start = ((), (), s32[]{:S(2)}) async-start(), calls=%async_computation.5 | async-start | bytes 1990656 | tf_op jit(solution)/shard_map/reduce_scatter | solution.py:178
Sparse Core Ops, SparseCore 0:
  210.8 38.7 reduce-scatter.6
  252.6 36.3 reduce-scatter.4

commit v2 on v1

--- a/solution.py
+++ b/solution.py
@@ -106,16 +106,21 @@
     d_tokens_ref[...] = result.reshape(d_tokens_ref.shape).astype(jnp.bfloat16)
 
 
+def mask_of(live_slots, rows, group):
+    at = jnp.arange(rows, dtype=jnp.int32)
+    live_rows = jnp.repeat(live_slots, group)
+    mask = jnp.where(
+        (at[:, None] % group == at[None, :] % group) & (live_rows[None, :] > 0.5), 0.0, -1e30
+    ).astype(jnp.float32)
+    return live_rows, mask
+
+
 def local_part(tokens, d_out, live_slots, w_qkv, w_out):
     slot_count, stripe, width = tokens.shape
     group = min(GROUP, stripe)
     rows = slot_count * group
     steps = stripe // group
-    at = jnp.arange(rows, dtype=jnp.int32)
-    live_rows = jnp.repeat(live_slots, group)
-    mask = jnp.where(
-        (at[:, None] % group == at[None, :] % group) & (live_rows[None, :] > 0.5), 0.0, -1e30
-    ).astype(jnp.float32)
+    live_rows, mask = mask_of(live_slots, rows, group)
     if steps == 1:
         tokens, d_out = tokens.reshape(rows, width), d_out.reshape(rows, width)
         moving = pl.BlockSpec((rows, width), lambda i: (0, 0))
@@ -154,6 +159,321 @@
     return d_tokens.reshape(slot_count, stripe, width), grad
 
 
+def exchange_kernel(
+    score_scale,
+    seq_size,
+    dp_size,
+    tokens_ref,
+    d_out_ref,
+    live_ref,
+    mask_ref,
+    w_qkv_hbm,
+    w_out_hbm,
+    d_tokens_ref,
+    final_ref,
+    w_qkv_ref,
+    w_out_ref,
+    got_tokens,
+    got_d_out,
+    results,
+    joined,
+    head_grad,
+    attended,
+    qkv_grad,
+    grad,
+    pair_sent,
+    pair_got,
+    dp_sent,
+    dp_got,
+    chip_sent,
+    chip_got,
+    weight_sems,
+    tokens_send,
+    tokens_recv,
+    d_out_send,
+    d_out_recv,
+    back_send,
+    back_recv,
+    pair_sems,
+    dp_send,
+    dp_recv,
+    chip_send,
+    chip_recv,
+):
+    rows, width = attended.shape
+    steps, slot_count, group, _ = got_tokens.shape
+    slots = tokens_ref.shape[0]
+    stripe = steps * group
+    chips = seq_size // 2
+    row_block, column_block = final_ref.shape
+    me = lax.axis_index("seq")
+    my_dp = lax.axis_index("dp")
+    core = lax.rem(me, 2)
+    chip = me // 2
+
+    def peer(k):
+        return lax.rem(me + k, seq_size)
+
+    def dp_peer(k):
+        return lax.rem(my_dp + k, dp_size)
+
+    barrier = pltpu.get_barrier_semaphore()
+    for k in range(1, seq_size):
+        pl.semaphore_signal(
+            barrier,
+            inc=1,
+            device_id={"seq": peer(k)},
+            device_id_type=pl.DeviceIdType.MESH,
+        )
+    for k in range(1, dp_size):
+        pl.semaphore_signal(
+            barrier,
+            inc=1,
+            device_id={"dp": dp_peer(k)},
+            device_id_type=pl.DeviceIdType.MESH,
+        )
+    weights = (
+        pltpu.make_async_copy(w_qkv_hbm, w_qkv_ref, weight_sems.at[0]),
+        pltpu.make_async_copy(w_out_hbm, w_out_ref, weight_sems.at[1]),
+    )
+    for copy in weights:
+        copy.start()
+    pl.semaphore_wait(barrier, seq_size - 1 + dp_size - 1)
+
+    def remote(source, target, send, recv, device):
+        return pltpu.make_async_remote_copy(
+            src_ref=source,
+            dst_ref=target,
+            send_sem=send,
+            recv_sem=recv,
+            device_id=device,
+            device_id_type=pl.DeviceIdType.MESH,
+        )
+
+    def home(ref, owner, g):
+        return ref.at[:, pl.ds(pl.multiple_of(owner * stripe + g * group, group), group), :]
+
+    def away(ref, owner, g):
+        return ref.at[g, pl.ds(owner * slots, slots)]
+
+    def spread(source, target, send, recv, g, k):
+        return remote(
+            home(source, peer(k), g),
+            away(target, me, g),
+            send.at[g, k],
+            recv.at[g, k],
+            {"seq": peer(k)},
+        )
+
+    def keep_own(source, target, recv, g):
+        return pltpu.make_async_copy(home(source, me, g), away(target, me, g), recv.at[g, 0])
+
+    def back(g, k):
+        return remote(
+            away(results, peer(k), g),
+            home(d_tokens_ref, me, g),
+            back_send.at[g, k],
+            back_recv.at[g, k],
+            {"seq": peer(k)},
+        )
+
+    def back_own(g):
+        return pltpu.make_async_copy(
+            away(results, me, g), home(d_tokens_ref, me, g), back_recv.at[g, 0]
+        )
+
+    moved = (
+        (tokens_ref, got_tokens, tokens_send, tokens_recv),
+        (d_out_ref, got_d_out, d_out_send, d_out_recv),
+    )
+
+    @pl.loop(0, steps)
+    def _(g):
+        for source, target, send, recv in moved:
+            for k in range(1, seq_size):
+                spread(source, target, send, recv, g, k).start()
+            keep_own(source, target, recv, g).start()
+
+    def arrived(which, g):
+        source, target, send, recv = moved[which]
+        for k in range(1, seq_size):
+            spread(source, target, send, recv, g, k).wait_recv()
+        keep_own(source, target, recv, g).wait()
+
+    for copy in weights:
+        copy.wait()
+    grad[...] = jnp.zeros_like(grad)
+
+    def pair_copy():
+        return remote(
+            pair_sent, pair_got, pair_sems.at[0], pair_sems.at[1], {"seq": chip * 2 + 1 - core}
+        )
+
+    def row_piece(at, parity):
+        start = pl.multiple_of((at * 2 + parity) * row_block, row_block)
+        return grad[pl.ds(start, row_block), :]
+
+    def columns_of(value, d):
+        return value[:, d * column_block : (d + 1) * column_block]
+
+    @pl.loop(0, steps)
+    def _(g):
+        arrived(0, g)
+        values = got_tokens[g].astype(jnp.float32).reshape(rows, width)
+        center = values - jnp.mean(values, axis=-1, keepdims=True)
+        inverse = lax.rsqrt(jnp.mean(center * center, axis=-1, keepdims=True) + 1e-06)
+        normalized = center * inverse
+        joined[...] = dot(normalized.astype(jnp.bfloat16), w_qkv_ref[...]).astype(jnp.bfloat16)
+        arrived(1, g)
+        masked_wide = got_d_out[g].astype(jnp.float32).reshape(rows, width) * live_ref[...]
+        masked = masked_wide.astype(jnp.bfloat16)
+        head_grad[...] = dot(masked, w_out_ref[...], NT).astype(jnp.bfloat16)
+        attend(joined, head_grad, mask_ref[...], attended, qkv_grad, width, score_scale)
+        grad[...] += dot(attended[...], masked, TN)
+
+        @pl.when(g == steps - 1)
+        def _():
+            @pl.loop(0, chips)
+            def _(at):
+                value = row_piece(at, 1 - core)
+                for d in range(dp_size):
+                    pair_sent[d, at] = columns_of(value, d).astype(jnp.bfloat16)
+
+            pair_copy().start()
+
+        normed_grad = dot(qkv_grad[...], w_qkv_ref[...], NT)
+        mean_grad = jnp.mean(normed_grad, axis=-1, keepdims=True)
+        mean_cross = jnp.mean(normed_grad * normalized, axis=-1, keepdims=True)
+        result = masked_wide + inverse * (normed_grad - mean_grad - normalized * mean_cross)
+        results[g] = result.reshape(slot_count, group, width).astype(jnp.bfloat16)
+        for k in range(1, seq_size):
+            back(g, k).start()
+        back_own(g).start()
+
+    pair_copy().wait_recv()
+
+    @pl.loop(0, chips)
+    def _(at):
+        value = row_piece(at, core)
+        for d in range(dp_size):
+            total = columns_of(value, d) + pair_got[d, at].astype(jnp.float32)
+            dp_sent[d, at] = total.astype(jnp.bfloat16)
+
+    def dp_copy(k):
+        return remote(
+            dp_sent.at[dp_peer(k)],
+            dp_got.at[k - 1],
+            dp_send.at[k - 1],
+            dp_recv.at[k - 1],
+            {"dp": dp_peer(k)},
+        )
+
+    for k in range(1, dp_size):
+        dp_copy(k).start()
+    for k in range(1, dp_size):
+        dp_copy(k).wait_recv()
+
+    @pl.loop(0, chips)
+    def _(at):
+        total = dp_sent[my_dp, at].astype(jnp.float32)
+        for k in range(1, dp_size):
+            total = total + dp_got[k - 1, at].astype(jnp.float32)
+        chip_sent[at] = total.astype(jnp.bfloat16)
+
+    def chip_copy(k):
+        target = lax.rem(chip + k, chips)
+        return remote(
+            chip_sent.at[target],
+            chip_got.at[k - 1],
+            chip_send.at[k - 1],
+            chip_recv.at[k - 1],
+            {"seq": target * 2 + core},
+        )
+
+    for k in range(1, chips):
+        chip_copy(k).start()
+    total = chip_sent[chip].astype(jnp.float32)
+    for k in range(1, chips):
+        chip_copy(k).wait_recv()
+        total = total + chip_got[k - 1].astype(jnp.float32)
+    final_ref[...] = total
+
+    pair_copy().wait_send()
+    for k in range(1, dp_size):
+        dp_copy(k).wait_send()
+    for k in range(1, chips):
+        chip_copy(k).wait_send()
+
+    @pl.loop(0, steps)
+    def _(g):
+        for source, target, send, recv in moved:
+            for k in range(1, seq_size):
+                spread(source, target, send, recv, g, k).wait_send()
+        for k in range(1, seq_size):
+            back(g, k).wait()
+        back_own(g).wait()
+
+
+def exchange_part(tokens, d_out, live_slots, w_qkv, w_out, slots, seq_size, dp_size):
+    row_count, width = tokens.shape
+    slot_count = live_slots.shape[0]
+    stripe = row_count // slot_count
+    steps = stripe // GROUP
+    rows = slot_count * GROUP
+    chips = seq_size // 2
+    live_rows, mask = mask_of(live_slots, rows, GROUP)
+    tokens = tokens.reshape(slots, row_count // slots, width)
+    d_out = d_out.reshape(tokens.shape)
+    any_space = pl.BlockSpec(memory_space=pl.ANY)
+    vmem = pl.BlockSpec(memory_space=pltpu.VMEM)
+    narrow = jnp.bfloat16
+    parts = (chips, width // seq_size, width // dp_size)
+    crossing = pltpu.SemaphoreType.DMA((steps, seq_size))
+    d_tokens, final = pl.pallas_call(
+        functools.partial(exchange_kernel, 1.0 / math.sqrt(width // H), seq_size, dp_size),
+        in_specs=[any_space, any_space, vmem, vmem, any_space, any_space],
+        out_specs=[any_space, vmem],
+        out_shape=[
+            jax.ShapeDtypeStruct(tokens.shape, narrow),
+            jax.ShapeDtypeStruct(parts[1:], jnp.float32),
+        ],
+        scratch_shapes=[
+            pltpu.VMEM(w_qkv.shape, narrow),
+            pltpu.VMEM(w_out.shape, narrow),
+            pltpu.VMEM((steps, slot_count, GROUP, width), narrow),
+            pltpu.VMEM((steps, slot_count, GROUP, width), narrow),
+            pltpu.VMEM((steps, slot_count, GROUP, width), narrow),
+            pltpu.VMEM((rows, 3 * width), narrow),
+            pltpu.VMEM((rows, width), narrow),
+            pltpu.VMEM((rows, width), narrow),
+            pltpu.VMEM((rows, 3 * width), narrow),
+            pltpu.VMEM((width, width), jnp.float32),
+            pltpu.VMEM((dp_size, *parts), narrow),
+            pltpu.VMEM((dp_size, *parts), narrow),
+            pltpu.VMEM((dp_size, *parts), narrow),
+            pltpu.VMEM((dp_size - 1, *parts), narrow),
+            pltpu.VMEM(parts, narrow),
+            pltpu.VMEM((chips - 1, *parts[1:]), narrow),
+            pltpu.SemaphoreType.DMA((2,)),
+            crossing,
+            crossing,
+            crossing,
+            crossing,
+            crossing,
+            crossing,
+            pltpu.SemaphoreType.DMA((2,)),
+            pltpu.SemaphoreType.DMA((dp_size - 1,)),
+            pltpu.SemaphoreType.DMA((dp_size - 1,)),
+            pltpu.SemaphoreType.DMA((chips - 1,)),
+            pltpu.SemaphoreType.DMA((chips - 1,)),
+        ],
+        compiler_params=pltpu.CompilerParams(
+            collective_id=0, has_side_effects=True, vmem_limit_bytes=60 * 2**20
+        ),
+    )(tokens, d_out, live_rows[:, None], mask, w_qkv, w_out)
+    return d_tokens, final
+
+
 def body(tokens, d_out, frames, frame_order, w_qkv, w_out):
     _, row_count, width = tokens.shape
     seq_size = lax.axis_size("seq")
@@ -164,6 +484,20 @@
     piece = row_count // slots // seq_size
     live_slots = (frame_order[0] < frames[0]).astype(jnp.float32)
 
+    dp_size = lax.axis_size("dp")
+    if (
+        piece == stripe
+        and stripe % GROUP == 0
+        and seq_size % 2 == 0
+        and seq_size > 2
+        and dp_size > 1
+        and width % (16 * seq_size) == 0
+    ):
+        d_rows, final_out = exchange_part(
+            tokens[0], d_out[0], live_slots, w_qkv, w_out, slots, seq_size, dp_size
+        )
+        return (d_rows.reshape(tokens.shape), final_out)
+
     def spread(rows):
         sent = rows.reshape(slots, seq_size, piece, width)
         got = lax.all_to_all(sent, "seq", split_axis=1, concat_axis=0, tiled=True)

time: 296 us -> 182 us (0.61)
  waiting for transfers between devices: 174 us -> 0 us
  Pallas kernels: 74.1 us -> 173 us
  starting transfers between devices: 14.4 us -> 0 us
  between operations: 14.7 us -> 1.3 us
  local copies, waits for them, and re-layouts: 14.1 us -> 4.98 us
  other arithmetic: 4.96 us -> 1.48 us
    all_to_all x3 -> x0, waiting for transfers between devices: 129 us -> none  [the longest x2 103 us: spread(): got = lax.all_to_all(sent, 'seq', split_axis=1, concat_axis=0, tiled=True)]
    pallas_call x1, Pallas kernels: 74.1 us -> 173 us  [exchange_part(): pl.pallas_call(functools.partial(exchange_kernel, 1.0 / math.sqrt(width /...]
    unnamed x3 -> x0, waiting for transfers between devices: 35.3 us -> none
    all_to_all x3 -> x0, starting transfers between devices: 14.4 us -> none  [the longest x2 10.7 us: spread(): got = lax.all_to_all(sent, 'seq', split_axis=1, concat_axis=0, tiled=True)]
    reduce_scatter x1 -> x0, waiting for transfers between devices: 9.05 us -> none  [body(): final_out = lax.psum_scatter(share, 'seq', scatter_dimension=0, tiled=True)]
    reshape x2 -> x0, local copies, waits for them, and re-layouts: 6.65 us -> none  [spread(): sent = rows.reshape(slots, seq_size, piece, width)]
    convert_element_type x2 -> x0, other arithmetic: 4.12 us -> none  [the longest x1 2.77 us: body(): grad_out.astype(jnp.bfloat16)]
  transfers between devices with their start and end apart: 5 -> 0, of which waited for: 5 -> 0; matrix products, arithmetic and copies ran while one was open for 3% -> 0% of each run, Pallas kernels for 0% -> 0%
where the time goes in v2:
time: 182 us; the launch traced here: 181 us
  Pallas kernels  173 us (95%)
  local copies, waits for them, and re-layouts  4.98 us (3%)
    pallas_call x1, Pallas kernels, exchange_part(): pl.pallas_call(functools.partial(exchange_kernel, 1.0 / math.sqrt(width /...  173 us
    unnamed x4, local copies, waits for them, and re-layouts  3.98 us

profile of v2, /device:TPU:0, one launch (start us, length us, event | category | flops | bytes accessed | tf_op | source)
XLA Modules:
  0.0 181.2 jit_solution(15790219803360685995)
XLA Ops:
  1.3 0.7 broadcast_compare_fusion
  1.9 0.1 broadcast_in_dim.16
  2.0 0.1 gt.17
  2.1 0.1 broadcast_in_dim.15
  2.2 0.8 broadcast_in_dim_reshape.5.live_ref
  2.9 0.8 and_select_fusion.mask_ref
  3.8 173.4 %shard_map.77 = (bf16[4,256,1152]{2,1,0:T(8,128)(2,1)}, f32[144,288]{1,0:T(8,128)}) custom-call(bf16[4,256,1152]{2,1,0:T(8,128)(2,1)} %bitcast.9, bf16[4,256,1152]{2,1,0:T(8,128)(2,1)} %bitcast.10, f32[256,1]{1,0:T(8,128)} %broadcast_in_dim_reshape.5.live_ref, f32[256,256]{1,0:T(8,128)} %and_select_fusion.mask_ref, bf16[1152,3456]{1,0:T(8,128)(2,1)} %w_qkv_hbm.1, ...), custom_call_target="tpu_custom_call" | custom-call | tf_op jit(solution)/shard_map/pallas_call | solution.py:432
  177.2 0.0 copy-start
  177.2 3.3 %copy.12 = bf16[1,1024,1152]{2,1,0:T(8,128)(2,1)} copy(bf16[1,1024,1152]{2,1,0:T(8,128)(2,1)} %bitcast.8) | data formatting | bytes 4718592
  180.5 0.0 copy-done
  180.5 0.7 copy.13
  (1 shorter events, 0.0 us)
Async XLA Ops:
  177.2 3.3 %copy-start = (f32[144,288]{1,0:T(8,128)S(1)}, f32[144,288]{1,0:T(8,128)}, u32[]{:S(2)}) copy-start(f32[144,288]{1,0:T(8,128)} %get-tuple-element.11) | copy-start | bytes 497668

commit v3 on v2

--- a/solution.py
+++ b/solution.py
@@ -165,8 +165,8 @@
     dp_size,
     tokens_ref,
     d_out_ref,
-    live_ref,
-    mask_ref,
+    frames_ref,
+    order_ref,
     w_qkv_hbm,
     w_out_hbm,
     d_tokens_ref,
@@ -187,6 +187,8 @@
     dp_got,
     chip_sent,
     chip_got,
+    live_ref,
+    mask_ref,
     weight_sems,
     tokens_send,
     tokens_recv,
@@ -300,6 +302,15 @@
             spread(source, target, send, recv, g, k).wait_recv()
         keep_own(source, target, recv, g).wait()
 
+    live_row = jnp.where(order_ref[...] < frames_ref[0], 1.0, 0.0)
+    slot_of_row = lax.broadcasted_iota(jnp.int32, (rows, slot_count), 0) // group
+    slot = lax.broadcasted_iota(jnp.int32, (rows, slot_count), 1)
+    slot_hit = jnp.where(slot_of_row == slot, 1.0, 0.0)
+    live_ref[...] = jnp.sum(slot_hit * live_row, axis=-1, keepdims=True)
+    key_live = dot(live_row.astype(jnp.bfloat16), slot_hit.astype(jnp.bfloat16), NT)
+    patch = lax.broadcasted_iota(jnp.int32, (rows, rows), 0) % group
+    key_patch = lax.broadcasted_iota(jnp.int32, (rows, rows), 1) % group
+    mask_ref[...] = jnp.where((patch == key_patch) & (key_live > 0.5), 0.0, -1e30)
     for copy in weights:
         copy.wait()
     grad[...] = jnp.zeros_like(grad)
@@ -380,29 +391,48 @@
             total = total + dp_got[k - 1, at].astype(jnp.float32)
         chip_sent[at] = total.astype(jnp.bfloat16)
 
-    def chip_copy(k):
-        target = lax.rem(chip + k, chips)
+    def chip_copy(block, slot_at, target):
         return remote(
-            chip_sent.at[target],
-            chip_got.at[k - 1],
-            chip_send.at[k - 1],
-            chip_recv.at[k - 1],
+            chip_sent.at[block],
+            chip_got.at[slot_at],
+            chip_send.at[slot_at],
+            chip_recv.at[slot_at],
             {"seq": target * 2 + core},
         )
 
-    for k in range(1, chips):
-        chip_copy(k).start()
+    if chips == 4:
+        near = chip + 1 - 2 * lax.rem(chip, 2)
+        far = lax.rem(chip + 2, chips)
+        chip_copies = [
+            chip_copy(lax.rem(near + 2, chips), 0, near),
+            chip_copy(near, 1, near),
+            chip_copy(far, 2, far),
+        ]
+        chip_copies[0].start()
+        chip_copies[1].start()
+        chip_copies[0].wait_recv()
+        crossing = chip_sent[far].astype(jnp.float32) + chip_got[0].astype(jnp.float32)
+        chip_sent[far] = crossing.astype(jnp.bfloat16)
+        chip_copies[2].start()
+        arriving = (1, 2)
+    else:
+        chip_copies = []
+        for k in range(1, chips):
+            target = lax.rem(chip + k, chips)
+            chip_copies.append(chip_copy(target, k - 1, target))
+            chip_copies[-1].start()
+        arriving = range(chips - 1)
     total = chip_sent[chip].astype(jnp.float32)
-    for k in range(1, chips):
-        chip_copy(k).wait_recv()
-        total = total + chip_got[k - 1].astype(jnp.float32)
+    for slot_at in arriving:
+        chip_copies[slot_at].wait_recv()
+        total = total + chip_got[slot_at].astype(jnp.float32)
     final_ref[...] = total
 
     pair_copy().wait_send()
     for k in range(1, dp_size):
         dp_copy(k).wait_send()
-    for k in range(1, chips):
-        chip_copy(k).wait_send()
+    for copy in chip_copies:
+        copy.wait_send()
 
     @pl.loop(0, steps)
     def _(g):
@@ -414,24 +444,24 @@
         back_own(g).wait()
 
 
-def exchange_part(tokens, d_out, live_slots, w_qkv, w_out, slots, seq_size, dp_size):
+def exchange_part(tokens, d_out, frames, frame_order, w_qkv, w_out, slots, seq_size, dp_size):
     row_count, width = tokens.shape
-    slot_count = live_slots.shape[0]
+    slot_count = frame_order.shape[1]
     stripe = row_count // slot_count
     steps = stripe // GROUP
     rows = slot_count * GROUP
     chips = seq_size // 2
-    live_rows, mask = mask_of(live_slots, rows, GROUP)
     tokens = tokens.reshape(slots, row_count // slots, width)
     d_out = d_out.reshape(tokens.shape)
     any_space = pl.BlockSpec(memory_space=pl.ANY)
     vmem = pl.BlockSpec(memory_space=pltpu.VMEM)
+    smem = pl.BlockSpec(memory_space=pltpu.SMEM)
     narrow = jnp.bfloat16
     parts = (chips, width // seq_size, width // dp_size)
     crossing = pltpu.SemaphoreType.DMA((steps, seq_size))
     d_tokens, final = pl.pallas_call(
         functools.partial(exchange_kernel, 1.0 / math.sqrt(width // H), seq_size, dp_size),
-        in_specs=[any_space, any_space, vmem, vmem, any_space, any_space],
+        in_specs=[any_space, any_space, smem, vmem, any_space, any_space],
         out_specs=[any_space, vmem],
         out_shape=[
             jax.ShapeDtypeStruct(tokens.shape, narrow),
@@ -454,6 +484,8 @@
             pltpu.VMEM((dp_size - 1, *parts), narrow),
             pltpu.VMEM(parts, narrow),
             pltpu.VMEM((chips - 1, *parts[1:]), narrow),
+            pltpu.VMEM((rows, 1), jnp.float32),
+            pltpu.VMEM((rows, rows), jnp.float32),
             pltpu.SemaphoreType.DMA((2,)),
             crossing,
             crossing,
@@ -470,7 +502,7 @@
         compiler_params=pltpu.CompilerParams(
             collective_id=0, has_side_effects=True, vmem_limit_bytes=60 * 2**20
         ),
-    )(tokens, d_out, live_rows[:, None], mask, w_qkv, w_out)
+    )(tokens, d_out, frames, frame_order, w_qkv, w_out)
     return d_tokens, final
 
 
@@ -494,7 +526,7 @@
         and width % (16 * seq_size) == 0
     ):
         d_rows, final_out = exchange_part(
-            tokens[0], d_out[0], live_slots, w_qkv, w_out, slots, seq_size, dp_size
+            tokens[0], d_out[0], frames, frame_order, w_qkv, w_out, slots, seq_size, dp_size
         )
         return (d_rows.reshape(tokens.shape), final_out)
 

time: 182 us -> 183 us (level)
  Pallas kernels: 173 us -> 178 us
    pallas_call x1, Pallas kernels: 173 us -> 178 us  [exchange_part(): pl.pallas_call(functools.partial(exchange_kernel, 1.0 / math.sqrt(width /...]
where the time goes in v3:
time: 183 us
  Pallas kernels  178 us (97%)
  local copies, waits for them, and re-layouts  3.98 us (2%)
    pallas_call x1, Pallas kernels, exchange_part(): pl.pallas_call(functools.partial(exchange_kernel, 1.0 / math.sqrt(width /...  178 us
    unnamed x4, local copies, waits for them, and re-layouts  3.98 us

profile of v3, /device:TPU:0, one launch (start us, length us, event | category | flops | bytes accessed | tf_op | source)
XLA Modules:
  0.0 182.9 jit_solution(2647277266539713723)
XLA Ops:
  1.3 177.6 %shard_map.77 = (bf16[4,256,1152]{2,1,0:T(8,128)(2,1)}, f32[144,288]{1,0:T(8,128)}) custom-call(bf16[4,256,1152]{2,1,0:T(8,128)(2,1)} %bitcast.4, bf16[4,256,1152]{2,1,0:T(8,128)(2,1)} %bitcast.5, s32[1]{0:T(128)S(6)} %copy.10.frames_ref, s32[1,32]{1,0:T(1,128)} %order_ref.1, bf16[1152,3456]{1,0:T(8,128)(2,1)} %w_qkv_hbm.1, bf16[1152,1152]{1,0:T(8,128)(2,1)} %w_out_hbm.1), custom_call_target="tpu_custom_call" | custom-call | tf_op jit(solution)/shard_map/pallas_call | solution.py:462
  178.9 0.0 copy-start
  178.9 3.3 %copy.11 = bf16[1,1024,1152]{2,1,0:T(8,128)(2,1)} copy(bf16[1,1024,1152]{2,1,0:T(8,128)(2,1)} %bitcast.3) | data formatting | bytes 4718592
  182.2 0.0 copy-done
  182.2 0.7 copy.12
Async XLA Ops:
  178.9 3.3 %copy-start = (f32[144,288]{1,0:T(8,128)S(1)}, f32[144,288]{1,0:T(8,128)}, u32[]{:S(2)}) copy-start(f32[144,288]{1,0:T(8,128)} %get-tuple-element.9) | copy-start | bytes 497668
